TPU v7x, 128 devices: a whole 4x4x4 slice. The times are simulated.
128 devices in a mesh: mat: 8 (over x, core), frac: 16 (over z, y).
Axes of the slice: x: 4, y: 4, z: 4, core: 2. Of those that a mesh axis runs over, the one named last changes fastest.
Arguments:
- pressure_start: float32 [128, 1024, 256], P('mat', 'frac'), may hold values from -6 to 6
- face_trans: float32 [3, 128, 1024, 256], P(None, 'mat', 'frac'), may hold values from 0.2 to 2
- cell_coef: float32 [128, 1024, 256], P('mat', 'frac'), may hold values from 0.05 to 0.5
- matrix_source: float32 [128, 1024, 256], P('mat', 'frac'), may hold values from -6 to 6
- mortar_owner: int32 [65536, 1], P(('mat', 'frac')), may hold values from 0 to 127; in each aligned block of 512 rows (0 to 511, 512 to 1023, ...) at most 8 rows name the same one
- mortar_cell: int32 [65536], P(('mat', 'frac')), may hold values from 0 to 262143
- mortar_frac: int32 [65536], P(('mat', 'frac')), may hold values from 0 to 16383
- mortar_kappa: float32 [65536], P(('mat', 'frac')), may hold values from 0.5 to 2
- tiles: float32 [128, 4, 128, 128], P('frac'), may hold values from -0.25 to 0.25
- tile_cols: int32 [128, 4], P('frac'), may hold values from 0 to 127
- frac_diag: float32 [16384], P('frac'), may hold values from 4 to 8
- frac_source: float32 [16384], P('frac'), may hold values from -6 to 6
- fracture_start: float32 [16384], P('frac'), may hold values from -6 to 6
Outputs:
- pressure: float32 [128, 1024, 256], P('mat', 'frac')
- fracture: float32 [16384], P('frac')
- flux: float32 [65536], P(('mat', 'frac'))
Inputs may be any that keep to these rules, and one draw needn't show every extreme that they name: `mortar_owner`: among the 512 mortar cells of one device, at most 8 name the same owner, and in some devices some owner is named exactly 8 times.
All inputs are finite; a program needn't handle non-finite values.
Results may differ from a plain program's by a relative error of at most 0.00015.
Values sent between devices are 32-bit elements; how exact they have to be, the bound alone decides.
No kernel may reach another device: no remote copies, remote signals or barrier semaphores. Data moves between devices by JAX's collectives and lax.ppermute only.
A program may use at most 128 MiB of HBM per device.

v0:
```python
import jax
import jax.numpy as jnp
from jax import lax
from jax.sharding import PartitionSpec as P

SWEEPS = 2
CG_ITERS = 3
OUTER = 2
relax_weight = 0.8


def with_halo(block, sides, width):
    for axis, dim in sides:
        count = lax.axis_size(axis)
        forward = [(i, i + 1) for i in range(count - 1)]
        backward = [(target, source) for source, target in forward]
        low = lax.ppermute(
            lax.slice_in_dim(block, block.shape[dim] - width, None, axis=dim), axis, forward
        )
        high = lax.ppermute(lax.slice_in_dim(block, 0, width, axis=dim), axis, backward)
        block = jnp.concatenate([low, block, high], axis=dim)
    return block


def copy_for_each(x, axis):
    length = lax.axis_size(axis)
    return lax.all_to_all(jnp.broadcast_to(x[None], (length, *x.shape)), axis, 0, 0, tiled=True)


def in_order(blocks, dim):
    lengths = list(blocks.shape[1:])
    lengths[dim] *= blocks.shape[0]
    return jnp.moveaxis(blocks, 0, dim).reshape(lengths)


def gather_directly(x, axis, dim):
    blocks = copy_for_each(x, axis)
    return in_order(blocks, dim)


def split_up(x, dim, length):
    lengths = x.shape
    blocks = x.reshape(*lengths[:dim], length, lengths[dim] // length, *lengths[dim + 1 :])
    return jnp.moveaxis(blocks, dim, 0)


def summed_on_arrival(x, axis, dim):
    length = lax.axis_size(axis)
    blocks = lax.all_to_all(split_up(x, dim, length), axis, 0, 0, tiled=True)
    return jnp.sum(blocks, axis=0)


def of_everyone(x, axis):
    return copy_for_each(x, axis).sum(axis=0)


def in_one(arrays, axis):
    ends = [0]
    for a in arrays:
        ends.append(ends[-1] + a.size)
    running = of_everyone(jnp.concatenate([a.ravel() for a in arrays]), axis)
    return tuple((running[b:e].reshape(a.shape) for a, b, e in zip(arrays, ends, ends[1:])))


def shift_next(values, along):
    padding = [(0, 0)] * values.ndim
    padding[along] = (0, 1)
    return lax.slice_in_dim(jnp.pad(values, padding), 1, values.shape[along] + 1, axis=along)


def shift_prev(values, along):
    padding = [(0, 0)] * values.ndim
    padding[along] = (1, 0)
    return lax.slice_in_dim(jnp.pad(values, padding), 0, values.shape[along], axis=along)


def relax(padded, coef_part, source_part, inside):
    centre = padded[1:-1, 1:-1]
    tx_here = coef_part[0, 1:-1, 1:-1]
    tx_low = coef_part[0, :-2, 1:-1]
    ty_here = coef_part[1, 1:-1, 1:-1]
    ty_low = coef_part[1, 1:-1, :-2]
    tz_here = coef_part[2, 1:-1, 1:-1]
    tz_low = shift_prev(tz_here, 2)
    cell_part = coef_part[3, 1:-1, 1:-1]
    base_part = coef_part[4, 1:-1, 1:-1]
    diagonal = cell_part + tx_here + tx_low + ty_here + ty_low + tz_here + tz_low
    diagonal = jnp.where(inside, diagonal, 1.0)
    applied = (
        diagonal * centre
        - tx_here * padded[2:, 1:-1]
        - tx_low * padded[:-2, 1:-1]
        - ty_here * padded[1:-1, 2:]
        - ty_low * padded[1:-1, :-2]
        - tz_here * shift_next(centre, 2)
        - tz_low * shift_prev(centre, 2)
    )
    updated = centre + relax_weight * (base_part + source_part - applied) / diagonal
    return jnp.where(inside, updated, 0.0)


def body(
    pressure_start,
    face_trans,
    cell_coef,
    matrix_source,
    mortar_owner,
    mortar_cell,
    mortar_frac,
    mortar_kappa,
    tiles,
    tile_cols,
    frac_diag,
    frac_source,
    fracture_start,
):
    width_x, width_y, depth_z = pressure_start.shape
    cells = width_x * width_y * depth_z
    mat_count = lax.axis_size("mat")
    frac_count = lax.axis_size("frac")
    devices = mat_count * frac_count
    row_mat = lax.axis_index("mat")
    row_frac = lax.axis_index("frac")
    size_b = tiles.shape[2]
    coefs = jnp.concatenate([face_trans, cell_coef[None], matrix_source[None]], 0)
    coef_ext = with_halo(coefs, (("mat", 1), ("frac", 2)), SWEEPS)
    owner = mortar_owner[:, 0]
    mortar_count = owner.shape[0]
    capacity = max(2, 2 * mortar_count // devices)
    rows = jnp.arange(mortar_count, dtype=jnp.int32)
    earlier = (owner[:, None] == owner[None, :]) & (rows[None, :] < rows[:, None])
    slot = jnp.sum(earlier.astype(jnp.int32), axis=1)
    place = owner * capacity + slot
    index_slots = (
        jnp.full((devices * capacity,), cells, jnp.int32)
        .at[place]
        .set(mortar_cell)
        .reshape(devices, capacity)
    )
    asked = lax.all_to_all(index_slots, ("mat", "frac"), split_axis=0, concat_axis=0, tiled=True)
    asked_safe = jnp.minimum(asked, cells - 1)

    def fracture_apply(vector):
        whole = gather_directly(vector, "frac", 0)
        blocks = whole.reshape(-1, size_b)
        forward = jnp.einsum(
            "rtij,rtj->ri", tiles, blocks[tile_cols], precision=lax.Precision.HIGHEST
        )
        backward = jnp.einsum(
            "rtij,ri->rtj", tiles, vector.reshape(-1, size_b), precision=lax.Precision.HIGHEST
        )
        spread = jnp.zeros_like(blocks).at[tile_cols.reshape(-1)].add(backward.reshape(-1, size_b))
        returned = summed_on_arrival(spread, "frac", 0)
        return frac_diag * vector + 0.5 * (forward + returned).reshape(-1)

    def two_products(residual, image):
        return in_one((jnp.sum(residual * residual), jnp.sum(residual * image)), "frac")

    def solve_fracture(fracture, target):
        residual = target - fracture_apply(fracture)
        image = fracture_apply(residual)
        norm_now, product = two_products(residual, image)
        alpha = norm_now / product
        direction, along_image = (residual, image)
        for step in range(CG_ITERS):
            fracture = fracture + alpha * direction
            residual = residual - alpha * along_image
            if step + 1 < CG_ITERS:
                image = fracture_apply(residual)
                norm_next, product = two_products(residual, image)
                ratio = norm_next / norm_now
                alpha = norm_next / (product - ratio * norm_next / alpha)
                direction = residual + ratio * direction
                along_image = image + ratio * along_image
                norm_now = norm_next
        return fracture

    pressure = pressure_start
    fracture = fracture_start
    flux = jnp.zeros(mortar_kappa.shape, jnp.float32)
    for outer_no in range(OUTER):
        local_values = pressure.reshape(-1)[asked_safe]
        returned = lax.all_to_all(
            local_values, ("mat", "frac"), split_axis=0, concat_axis=0, tiled=True
        )
        trace = returned.reshape(-1)[place]
        fracture_whole = lax.all_gather(fracture, "frac", axis=0, tiled=True)
        flux = mortar_kappa * (trace - fracture_whole[mortar_frac])
        landed = jax.ops.segment_sum(flux, mortar_frac, num_segments=fracture_whole.shape[0])
        rows_part = summed_on_arrival(landed, "frac", 0)
        load = lax.psum(rows_part, "mat")
        fracture = solve_fracture(fracture, frac_source + load)
        flux_slots = (
            jnp.zeros((devices * capacity,), jnp.float32)
            .at[place]
            .set(flux)
            .reshape(devices, capacity)
        )
        arrived = lax.all_to_all(
            flux_slots, ("mat", "frac"), split_axis=0, concat_axis=0, tiled=True
        )
        source = jax.ops.segment_sum(
            arrived.reshape(-1), asked_safe.reshape(-1), num_segments=cells
        ).reshape(pressure.shape)
        stacked = with_halo(jnp.stack([pressure, source]), (("mat", 1), ("frac", 2)), SWEEPS)
        current = stacked[0]
        source_ext = stacked[1]
        for sweep_no in range(SWEEPS):
            span_x = current.shape[0]
            span_y = current.shape[1]
            coef_part = coef_ext[:, sweep_no : sweep_no + span_x, sweep_no : sweep_no + span_y]
            source_part = source_ext[
                sweep_no + 1 : sweep_no + span_x - 1, sweep_no + 1 : sweep_no + span_y - 1
            ]
            offset = SWEEPS - sweep_no - 1
            global_x = row_mat * width_x - offset + jnp.arange(span_x - 2)
            global_y = row_frac * width_y - offset + jnp.arange(span_y - 2)
            keep_x = (global_x >= 0) & (global_x < width_x * mat_count)
            keep_y = (global_y >= 0) & (global_y < width_y * frac_count)
            current = relax(
                current, coef_part, source_part, (keep_x[:, None] & keep_y[None, :])[:, :, None]
            )
        pressure = current
    return (pressure, fracture, flux)


def solution(mesh):
    in_specs = (
        P("mat", "frac", None),
        P(None, "mat", "frac", None),
        P("mat", "frac", None),
        P("mat", "frac", None),
        P(("mat", "frac"), None),
        P(("mat", "frac")),
        P(("mat", "frac")),
        P(("mat", "frac")),
        P("frac", None, None, None),
        P("frac", None),
        P("frac"),
        P("frac"),
        P("frac"),
    )
    out_specs = (P("mat", "frac", None), P("frac"), P(("mat", "frac")))
    return jax.shard_map(body, mesh=mesh, in_specs=in_specs, out_specs=out_specs, check_vma=False)
```

profile of v0, /device:TPU:32, one launch (start us, length us, event | category | flops | bytes accessed | tf_op | source)
XLA Modules:
  0.0 576.3 jit_solution(12743596823609701940)
XLA Ops:
  5.8 10.2 %all-to-all-start = ((s32[128,1,8]{2,1,0:T(1,128)}), s32[128,1,8]{2,1,0:T(1,128)S(1)}, u32[]{:S(2)}, u32[]{:S(2)}) async-start(s32[128,1,8]{2,1,0:T(1,128)} %bitcast.4), calls=%async_computation | async-start | bytes 131072 | tf_op jit(solution)/shard_map/all_to_all | solution.py:140
  30.4 6.2 %gather_fusion = f32[1024]{0:T(1024)S(1)} fusion(f32[262144]{0:T(1024)S(1)} %bitcast.374, s32[1024]{0:T(1024)S(1)} %broadcast_clamp_fusion), kind=kCustom, calls=%fused_computation | custom fusion | bytes 12288 | tf_op jit(solution)/shard_map/gather | solution.py:182
  37.2 9.9 %all-to-all-start.1 = ((f32[128,1,8]{2,1,0:T(1,128)}), f32[128,1,8]{2,1,0:T(1,128)S(1)}, u32[]{:S(2)}, u32[]{:S(2)}) async-start(f32[128,1,8]{2,1,0:T(1,128)} %bitcast.6), calls=%async_computation.1 | async-start | bytes 131072 | tf_op jit(solution)/shard_map/all_to_all | solution.py:183
  47.1 24.0 %all_gather.6 = f32[16384]{0:T(1024)S(1)} all-gather(f32[1024]{0:T(1024)S(1)} %copy-done.25), channel_id=1, replica_groups=mesh['mat'=8,'frac'=16] {'frac'}, dimensions={0}, use_global_device_ids=true | all-gather | bytes 69632 | tf_op jit(solution)/shard_map/all_gather | solution.py:187
  81.3 7.6 %all-to-all-start.2 = ((f32[128,1,8]{2,1,0:T(1,128)}), f32[128,1,8]{2,1,0:T(1,128)S(1)}, u32[]{:S(2)}, u32[]{:S(2)}) async-start(f32[128,1,8]{2,1,0:T(1,128)} %bitcast.7), calls=%async_computation.2 | async-start | bytes 131072 | tf_op jit(solution)/shard_map/all_to_all | solution.py:199
  89.7 8.3 %all-to-all-done.2 = f32[128,1,8]{2,1,0:T(1,128)S(1)} async-done(((f32[128,1,8]{2,1,0:T(1,128)}), f32[128,1,8]{2,1,0:T(1,128)S(1)}, u32[]{:S(2)}, u32[]{:S(2)}) %all-to-all-start.2) | async-done | bytes 4128 | tf_op jit(solution)/shard_map/all_to_all | solution.py:199
  98.7 4.5 all-to-all-start.5
  104.7 4.9 all-to-all-done.5
  109.6 4.8 all-to-all-start.6
  119.4 6.2 %scatter_custom_fusion.2 = f32[262144]{0:T(1024)S(1)} fusion(s32[1024]{0:T(1024)S(1)} %reshape.654, f32[1024]{0:T(1024)S(1)} %reshape.656, f32[]{:T(128)} %constant.26.clone.1), kind=kCustom, calls=%fused_computation.158 | custom fusion | flops 1024 | bytes 1048580 | tf_op jit(solution)/shard_map/scatter-add | solution.py:202
  127.5 7.3 %all-to-all-start.4 = ((f32[16,1,1024]{2,1,0:T(1,128)}), f32[16,1,1024]{2,1,0:T(1,128)S(1)}, u32[]{:S(2)}, u32[]{:S(2)}) async-start(f32[16,1,1024]{2,1,0:T(1,128)} %bitcast.26), calls=%async_computation.4 | async-start | bytes 131072 | tf_op jit(solution)/shard_map/all_to_all | solution.py:49
  136.6 4.4 all-to-all-done.4
  141.0 12.4 %psum.14 = f32[1024]{0:T(1024)S(1)} all-reduce(f32[1024]{0:T(1024)S(1)} %reduce_sum.265), channel_id=1, replica_groups=mesh['mat'=8,'frac'=16] {'mat'}, use_global_device_ids=true, to_apply=%region_6.0 | all-reduce | flops 1024 | bytes 8192 | tf_op jit(solution)/shard_map/psum | solution.py:191
  154.2 4.8 all-to-all-start.7
  165.3 4.8 all-to-all-start.8
  179.1 4.8 all-to-all-start.9
  185.7 4.2 all-to-all-done.9
  192.6 4.9 all-to-all-start.10
  203.8 4.8 all-to-all-start.11
  217.4 4.8 all-to-all-start.12
  223.5 4.8 all-to-all-done.12
  234.0 5.2 all-to-all-start.13
  245.5 4.8 all-to-all-start.14
  259.3 4.8 all-to-all-start.15
  275.4 4.9 all-to-all-start.18
  281.4 4.7 collective-permute-start.3
  289.2 5.4 collective-permute-done.2
  312.1 5.9 %fusion.32 = (f32[18,66,256]{2,1,0:T(8,128)S(1)}, f32[18,66,256]{2,1,0:T(8,128)}) fusion(f32[18,66,256]{2,1,0:T(8,128)S(1)} %slice.369, f32[18,66,256]{2,1,0:T(8,128)S(1)} %slice_bitcast_fusion.4, f32[20,68,256]{2,1,0:T(8,128)S(1)} %get-tuple-element.29, f32[5,20,68,256]{3,2,1,0:T(8,128)S(1)} %pad_maximum_fusion, f32[20,68,256]{2,1,0:T(8,128)S(1)} %get-tuple-element.28, ...), kind=kLoop, calls=%fused_computation.95 | loop fusion | flops 9427968 | bytes 23790756 | tf_op jit(solution)/shard_map/jit(_where)/select_n | solution.py:99
  319.2 4.5 fusion.66
  325.3 6.2 %gather_fusion.3 = f32[1024]{0:T(1024)S(1)} fusion(f32[262144]{0:T(1024)S(1)} %bitcast.375, s32[1024]{0:T(1024)S(1)} %broadcast_clamp_fusion), kind=kCustom, calls=%fused_computation.3 | custom fusion | bytes 12288 | tf_op jit(solution)/shard_map/gather | solution.py:182
  332.2 4.6 all-to-all-start.3
  336.7 24.4 %all_gather.7 = f32[16384]{0:T(1024)S(1)} all-gather(f32[1024]{0:T(1024)S(1)} %multiply_add_fusion.1), channel_id=1, replica_groups=mesh['mat'=8,'frac'=16] {'frac'}, dimensions={0}, use_global_device_ids=true | all-gather | bytes 69632 | tf_op jit(solution)/shard_map/all_gather | solution.py:187
  366.3 5.4 all-to-all-start.19
  378.3 9.4 %all-to-all-start.16 = ((f32[128,1,8]{2,1,0:T(1,128)}), f32[128,1,8]{2,1,0:T(1,128)S(1)}, u32[]{:S(2)}, u32[]{:S(2)}) async-start(f32[128,1,8]{2,1,0:T(1,128)} %bitcast.96), calls=%async_computation.16 | async-start | bytes 131072 | tf_op jit(solution)/shard_map/all_to_all | solution.py:199
  396.9 4.5 all-to-all-start.17
  402.3 7.2 %scatter_custom_fusion.9 = f32[262144]{0:T(1024)} fusion(s32[1024]{0:T(1024)} %copy-done.47, f32[1024]{0:T(1024)S(1)} %reshape.712, f32[]{:T(128)} %constant.26.clone.1), kind=kCustom, calls=%fused_computation.156 | custom fusion | flops 1024 | bytes 1049088 | tf_op jit(solution)/shard_map/scatter-add | solution.py:202
  414.0 14.1 %psum.15 = f32[1024]{0:T(1024)S(1)} all-reduce(f32[1024]{0:T(1024)S(1)} %reduce_sum.279), channel_id=1, replica_groups=mesh['mat'=8,'frac'=16] {'mat'}, use_global_device_ids=true, to_apply=%region_28.29 | all-reduce | flops 1024 | bytes 8192 | tf_op jit(solution)/shard_map/psum | solution.py:191
  428.7 7.2 %all-to-all-start.20 = ((f32[16,1,1024]{2,1,0:T(1,128)}), f32[16,1,1024]{2,1,0:T(1,128)S(1)}, u32[]{:S(2)}, u32[]{:S(2)}) async-start(f32[16,1,1024]{2,1,0:T(1,128)} %broadcast_in_dim.112), calls=%async_computation.20 | async-start | bytes 131072 | tf_op jit(solution)/shard_map/all_to_all | solution.py:27
  442.2 4.8 all-to-all-start.21
  455.9 4.8 all-to-all-start.22
  462.0 4.8 all-to-all-done.22
  469.3 5.1 all-to-all-start.23
  480.7 4.8 all-to-all-start.24
  494.4 4.8 all-to-all-start.25
  510.9 4.9 all-to-all-start.26
  522.1 4.8 all-to-all-start.27
  535.3 10.7 %all_to_all.187 = f32[16,1,2]{2,1,0:T(1,128)S(1)} all-to-all(f32[16,1,2]{2,1,0:T(1,128)S(1)} %broadcast_in_dim.217), channel_id=1, replica_groups=mesh['mat'=8,'frac'=16] {'frac'}, dimensions={0} | all-to-all | bytes 256 | tf_op jit(solution)/shard_map/all_to_all | solution.py:27
  558.2 5.9 %collective-permute-done.10 = f32[2,20,2,256]{3,2,1,0:T(2,128)S(1)} collective-permute-done((f32[2,20,2,256]{3,2,1,0:T(2,128)S(1)}, f32[2,20,2,256]{3,2,1,0:T(2,128)S(1)}, u32[]{:S(2)}, u32[]{:S(2)}) %collective-permute-start.10) | collective-permute-done | bytes 81952 | tf_op jit(solution)/shard_map/ppermute | solution.py:17
  (309 shorter events, 228.4 us)
Async XLA Ops:
  2.4 75.7 %copy-start.43 = (s32[512,1]{0,1:T(1,128)}, s32[512,1]{0,1:T(1,128)S(1)}, u32[]{:S(2)}) copy-start(s32[512,1]{0,1:T(1,128)S(1)} %compare_select_fusion.1) | copy-start | bytes 6148
  5.8 24.3 %all-to-all-start = ((s32[128,1,8]{2,1,0:T(1,128)}), s32[128,1,8]{2,1,0:T(1,128)S(1)}, u32[]{:S(2)}, u32[]{:S(2)}) async-start(s32[128,1,8]{2,1,0:T(1,128)} %bitcast.4), calls=%async_computation | async-start | bytes 131072 | tf_op jit(solution)/shard_map/all_to_all | solution.py:140
  18.6 277.3 %collective-permute-start.5 = (f32[5,2,64,256]{3,2,1,0:T(8,128)}, f32[5,2,64,256]{3,2,1,0:T(8,128)}, u32[]{:S(2)}, u32[]{:S(2)}) collective-permute-start(f32[5,2,64,256]{3,2,1,0:T(8,128)} %get-tuple-element.25), channel_id=1, source_target_pairs={{16,0},{32,16},{48,32},{64,48},{80,64},{96,80},{112,96},{17,1},{33... | collective-permute-start | bytes 1966088 | tf_op jit(solution)/shard_map/ppermute | solution.py:20
  20.0 275.9 %collective-permute-start.4 = (f32[5,2,64,256]{3,2,1,0:T(8,128)}, f32[5,2,64,256]{3,2,1,0:T(8,128)}, u32[]{:S(2)}, u32[]{:S(2)}) collective-permute-start(f32[5,2,64,256]{3,2,1,0:T(8,128)} %get-tuple-element.24), channel_id=1, source_target_pairs={{0,16},{16,32},{32,48},{48,64},{64,80},{80,96},{96,112},{1,17},{17... | collective-permute-start | bytes 1966088 | tf_op jit(solution)/shard_map/ppermute | solution.py:17
  23.9 51.9 %copy-start.39 = (s32[1024]{0:T(1024)}, s32[1024]{0:T(1024)S(1)}, u32[]{:S(2)}) copy-start(s32[1024]{0:T(1024)S(1)} %pad_clamp_fusion.2) | copy-start | bytes 12292
  26.3 44.9 %copy-start.41 = (s32[1024]{0:T(1024)}, s32[1024]{0:T(1024)S(1)}, u32[]{:S(2)}) copy-start(s32[1024]{0:T(1024)S(1)} %pad_clamp_fusion.1) | copy-start | bytes 12292
  37.2 37.0 %all-to-all-start.1 = ((f32[128,1,8]{2,1,0:T(1,128)}), f32[128,1,8]{2,1,0:T(1,128)S(1)}, u32[]{:S(2)}, u32[]{:S(2)}) async-start(f32[128,1,8]{2,1,0:T(1,128)} %bitcast.6), calls=%async_computation.1 | async-start | bytes 131072 | tf_op jit(solution)/shard_map/all_to_all | solution.py:183
  81.3 16.7 %all-to-all-start.2 = ((f32[128,1,8]{2,1,0:T(1,128)}), f32[128,1,8]{2,1,0:T(1,128)S(1)}, u32[]{:S(2)}, u32[]{:S(2)}) async-start(f32[128,1,8]{2,1,0:T(1,128)} %bitcast.7), calls=%async_computation.2 | async-start | bytes 131072 | tf_op jit(solution)/shard_map/all_to_all | solution.py:199
  98.7 10.8 %all-to-all-start.5 = ((f32[16,1,1024]{2,1,0:T(1,128)}), f32[16,1,1024]{2,1,0:T(1,128)S(1)}, u32[]{:S(2)}, u32[]{:S(2)}) async-start(f32[16,1,1024]{2,1,0:T(1,128)} %broadcast_in_dim.103), calls=%async_computation.5 | async-start | bytes 131072 | tf_op jit(solution)/shard_map/all_to_all | solution.py:27
  103.2 137.1 %copy-start.50 = (s32[32]{0:T(128)}, s32[32]{0:T(128)S(1)}, u32[]{:S(2)}) copy-start(s32[32]{0:T(128)S(1)} %fusion.103) | copy-start | bytes 388
  109.6 17.9 %all-to-all-start.6 = ((f32[16,8,128]{2,1,0:T(8,128)}), f32[16,8,128]{2,1,0:T(8,128)S(1)}, u32[]{:S(2)}, u32[]{:S(2)}) async-start(f32[16,8,128]{2,1,0:T(8,128)} %bitcast.40), calls=%async_computation.6 | async-start | bytes 131072 | tf_op jit(solution)/shard_map/all_to_all | solution.py:49
  127.5 13.5 %all-to-all-start.4 = ((f32[16,1,1024]{2,1,0:T(1,128)}), f32[16,1,1024]{2,1,0:T(1,128)S(1)}, u32[]{:S(2)}, u32[]{:S(2)}) async-start(f32[16,1,1024]{2,1,0:T(1,128)} %bitcast.26), calls=%async_computation.4 | async-start | bytes 131072 | tf_op jit(solution)/shard_map/all_to_all | solution.py:49
  153.5 38.4 %copy-start.23 = (f32[1024]{0:T(1024)}, f32[1024]{0:T(1024)S(1)}, u32[]{:S(2)}) copy-start(f32[1024]{0:T(1024)S(1)} %fusion.96) | copy-start | bytes 12292
  154.2 11.1 %all-to-all-start.7 = ((f32[16,1,1024]{2,1,0:T(1,128)}), f32[16,1,1024]{2,1,0:T(1,128)S(1)}, u32[]{:S(2)}, u32[]{:S(2)}) async-start(f32[16,1,1024]{2,1,0:T(1,128)} %broadcast_in_dim.105), calls=%async_computation.7 | async-start | bytes 131072 | tf_op jit(solution)/shard_map/all_to_all | solution.py:27
  165.3 11.1 %all-to-all-start.8 = ((f32[16,8,128]{2,1,0:T(8,128)}), f32[16,8,128]{2,1,0:T(8,128)S(1)}, u32[]{:S(2)}, u32[]{:S(2)}) async-start(f32[16,8,128]{2,1,0:T(8,128)} %bitcast.55), calls=%async_computation.8 | async-start | bytes 131072 | tf_op jit(solution)/shard_map/all_to_all | solution.py:49
  179.1 10.8 %all-to-all-start.9 = ((f32[16,1,2]{2,1,0:T(1,128)}), f32[16,1,2]{2,1,0:T(1,128)S(1)}, u32[]{:S(2)}, u32[]{:S(2)}) async-start(f32[16,1,2]{2,1,0:T(1,128)} %broadcast_in_dim.106), calls=%async_computation.9 | async-start | bytes 16384 | tf_op jit(solution)/shard_map/all_to_all | solution.py:27
  192.6 11.2 %all-to-all-start.10 = ((f32[16,1,1024]{2,1,0:T(1,128)}), f32[16,1,1024]{2,1,0:T(1,128)S(1)}, u32[]{:S(2)}, u32[]{:S(2)}) async-start(f32[16,1,1024]{2,1,0:T(1,128)} %broadcast_in_dim.107), calls=%async_computation.10 | async-start | bytes 131072 | tf_op jit(solution)/shard_map/all_to_all | solution.py:27
  203.8 11.1 %all-to-all-start.11 = ((f32[16,8,128]{2,1,0:T(8,128)}), f32[16,8,128]{2,1,0:T(8,128)S(1)}, u32[]{:S(2)}, u32[]{:S(2)}) async-start(f32[16,8,128]{2,1,0:T(8,128)} %bitcast.73), calls=%async_computation.11 | async-start | bytes 131072 | tf_op jit(solution)/shard_map/all_to_all | solution.py:49
  217.4 10.8 %all-to-all-start.12 = ((f32[16,1,2]{2,1,0:T(1,128)}), f32[16,1,2]{2,1,0:T(1,128)S(1)}, u32[]{:S(2)}, u32[]{:S(2)}) async-start(f32[16,1,2]{2,1,0:T(1,128)} %broadcast_in_dim.108), calls=%async_computation.12 | async-start | bytes 16384 | tf_op jit(solution)/shard_map/all_to_all | solution.py:27
  222.2 58.1 %collective-permute-start.1 = (f32[2,2,64,256]{3,2,1,0:T(8,128)}, f32[2,2,64,256]{3,2,1,0:T(8,128)S(1)}, u32[]{:S(2)}, u32[]{:S(2)}) collective-permute-start(f32[2,2,64,256]{3,2,1,0:T(8,128)} %get-tuple-element.37), channel_id=1, source_target_pairs={{16,0},{32,16},{48,32},{64,48},{80,64},{96,80},{112,96},{17,1},{33... | collective-permute-start | bytes 786440 | tf_op jit(solution)/shard_map/ppermute | solution.py:20
  234.0 11.4 %all-to-all-start.13 = ((f32[16,1,1024]{2,1,0:T(1,128)}), f32[16,1,1024]{2,1,0:T(1,128)S(1)}, u32[]{:S(2)}, u32[]{:S(2)}) async-start(f32[16,1,1024]{2,1,0:T(1,128)} %broadcast_in_dim.109), calls=%async_computation.13 | async-start | bytes 131072 | tf_op jit(solution)/shard_map/all_to_all | solution.py:27
  245.5 11.1 %all-to-all-start.14 = ((f32[16,8,128]{2,1,0:T(8,128)}), f32[16,8,128]{2,1,0:T(8,128)S(1)}, u32[]{:S(2)}, u32[]{:S(2)}) async-start(f32[16,8,128]{2,1,0:T(8,128)} %bitcast.91), calls=%async_computation.14 | async-start | bytes 131072 | tf_op jit(solution)/shard_map/all_to_all | solution.py:49
  259.3 10.8 %all-to-all-start.15 = ((f32[16,1,2]{2,1,0:T(1,128)}), f32[16,1,2]{2,1,0:T(1,128)S(1)}, u32[]{:S(2)}, u32[]{:S(2)}) async-start(f32[16,1,2]{2,1,0:T(1,128)} %broadcast_in_dim.110), calls=%async_computation.15 | async-start | bytes 16384 | tf_op jit(solution)/shard_map/all_to_all | solution.py:27
  264.0 16.3 %collective-permute-start = (f32[2,2,64,256]{3,2,1,0:T(8,128)}, f32[2,2,64,256]{3,2,1,0:T(8,128)}, u32[]{:S(2)}, u32[]{:S(2)}) collective-permute-start(f32[2,2,64,256]{3,2,1,0:T(8,128)} %get-tuple-element.36), channel_id=1, source_target_pairs={{0,16},{16,32},{32,48},{48,64},{64,80},{80,96},{96,112},{1,17},{17... | collective-permute-start | bytes 786440 | tf_op jit(solution)/shard_map/ppermute | solution.py:17
  274.7 153.3 %copy-start.21 = (f32[1024]{0:T(1024)}, f32[1024]{0:T(1024)S(1)}, u32[]{:S(2)}) copy-start(f32[1024]{0:T(1024)S(1)} %multiply_add_fusion.1) | copy-start | bytes 12292
  275.4 56.8 %all-to-all-start.18 = ((f32[16,1,1024]{2,1,0:T(1,128)}), f32[16,1,1024]{2,1,0:T(1,128)S(1)}, u32[]{:S(2)}, u32[]{:S(2)}) async-start(f32[16,1,1024]{2,1,0:T(1,128)} %broadcast_in_dim.111), calls=%async_computation.18 | async-start | bytes 131072 | tf_op jit(solution)/shard_map/all_to_all | solution.py:27
  281.4 7.8 %collective-permute-start.3 = (f32[2,20,2,256]{3,2,1,0:T(2,128)S(1)}, f32[2,20,2,256]{3,2,1,0:T(2,128)S(1)}, u32[]{:S(2)}, u32[]{:S(2)}) collective-permute-start(f32[2,20,2,256]{3,2,1,0:T(2,128)S(1)} %get-tuple-element.33), channel_id=1, source_target_pairs={{1,0},{2,1},{3,2},{4,3},{5,4},{6,5},{7,6},{8,7},{9,8},{10,9},{11,1... | collective-permute-start | bytes 245768 | tf_op jit(solution)/shard_map/ppermute | solution.py:20
  286.1 8.4 %collective-permute-start.2 = (f32[2,20,2,256]{3,2,1,0:T(2,128)S(1)}, f32[2,20,2,256]{3,2,1,0:T(2,128)S(1)}, u32[]{:S(2)}, u32[]{:S(2)}) collective-permute-start(f32[2,20,2,256]{3,2,1,0:T(2,128)S(1)} %get-tuple-element.32), channel_id=1, source_target_pairs={{0,1},{1,2},{2,3},{3,4},{4,5},{5,6},{6,7},{7,8},{8,9},{9,10},{10,1... | collective-permute-start | bytes 245768 | tf_op jit(solution)/shard_map/ppermute | solution.py:17
  297.1 7.7 %collective-permute-start.7 = (f32[5,20,2,256]{3,2,1,0:T(2,128)S(1)}, f32[5,20,2,256]{3,2,1,0:T(2,128)S(1)}, u32[]{:S(2)}, u32[]{:S(2)}) collective-permute-start(f32[5,20,2,256]{3,2,1,0:T(2,128)S(1)} %get-tuple-element.23), channel_id=1, source_target_pairs={{1,0},{2,1},{3,2},{4,3},{5,4},{6,5},{7,6},{8,7},{9,8},{10,9},{11,1... | collective-permute-start | bytes 614408 | tf_op jit(solution)/shard_map/ppermute | solution.py:20
  299.1 9.8 %collective-permute-start.6 = (f32[5,20,2,256]{3,2,1,0:T(2,128)S(1)}, f32[5,20,2,256]{3,2,1,0:T(2,128)S(1)}, u32[]{:S(2)}, u32[]{:S(2)}) collective-permute-start(f32[5,20,2,256]{3,2,1,0:T(2,128)S(1)} %get-tuple-element.22), channel_id=1, source_target_pairs={{0,1},{1,2},{2,3},{3,4},{4,5},{5,6},{6,7},{7,8},{8,9},{9,10},{10,1... | collective-permute-start | bytes 614408 | tf_op jit(solution)/shard_map/ppermute | solution.py:17
  325.3 35.9 %copy-start.42 = (s32[1024]{0:T(1024)S(1)}, s32[1024]{0:T(1024)}, u32[]{:S(2)}) copy-start(s32[1024]{0:T(1024)} %copy-done.41) | copy-start | bytes 12292
  331.4 41.2 %copy-start.40 = (s32[1024]{0:T(1024)S(1)}, s32[1024]{0:T(1024)}, u32[]{:S(2)}) copy-start(s32[1024]{0:T(1024)} %copy-done.39) | copy-start | bytes 12292
  332.2 34.1 %all-to-all-start.3 = ((f32[128,1,8]{2,1,0:T(1,128)}), f32[128,1,8]{2,1,0:T(1,128)S(1)}, u32[]{:S(2)}, u32[]{:S(2)}) async-start(f32[128,1,8]{2,1,0:T(1,128)} %bitcast.25), calls=%async_computation.3 | async-start | bytes 131072 | tf_op jit(solution)/shard_map/all_to_all | solution.py:183
  366.3 12.0 %all-to-all-start.19 = ((f32[16,8,128]{2,1,0:T(8,128)}), f32[16,8,128]{2,1,0:T(8,128)S(1)}, u32[]{:S(2)}, u32[]{:S(2)}) async-start(f32[16,8,128]{2,1,0:T(8,128)} %bitcast.112), calls=%async_computation.19 | async-start | bytes 131072 | tf_op jit(solution)/shard_map/all_to_all | solution.py:49
  378.3 18.6 %all-to-all-start.16 = ((f32[128,1,8]{2,1,0:T(1,128)}), f32[128,1,8]{2,1,0:T(1,128)S(1)}, u32[]{:S(2)}, u32[]{:S(2)}) async-start(f32[128,1,8]{2,1,0:T(1,128)} %bitcast.96), calls=%async_computation.16 | async-start | bytes 131072 | tf_op jit(solution)/shard_map/all_to_all | solution.py:199
  396.9 17.1 %all-to-all-start.17 = ((f32[16,1,1024]{2,1,0:T(1,128)}), f32[16,1,1024]{2,1,0:T(1,128)S(1)}, u32[]{:S(2)}, u32[]{:S(2)}) async-start(f32[16,1,1024]{2,1,0:T(1,128)} %bitcast.99), calls=%async_computation.17 | async-start | bytes 131072 | tf_op jit(solution)/shard_map/all_to_all | solution.py:49
  428.7 13.5 %all-to-all-start.20 = ((f32[16,1,1024]{2,1,0:T(1,128)}), f32[16,1,1024]{2,1,0:T(1,128)S(1)}, u32[]{:S(2)}, u32[]{:S(2)}) async-start(f32[16,1,1024]{2,1,0:T(1,128)} %broadcast_in_dim.112), calls=%async_computation.20 | async-start | bytes 131072 | tf_op jit(solution)/shard_map/all_to_all | solution.py:27
  442.2 11.1 %all-to-all-start.21 = ((f32[16,8,128]{2,1,0:T(8,128)}), f32[16,8,128]{2,1,0:T(8,128)S(1)}, u32[]{:S(2)}, u32[]{:S(2)}) async-start(f32[16,8,128]{2,1,0:T(8,128)} %bitcast.127), calls=%async_computation.21 | async-start | bytes 131072 | tf_op jit(solution)/shard_map/all_to_all | solution.py:49
  455.9 10.8 %all-to-all-start.22 = ((f32[16,1,2]{2,1,0:T(1,128)}), f32[16,1,2]{2,1,0:T(1,128)S(1)}, u32[]{:S(2)}, u32[]{:S(2)}) async-start(f32[16,1,2]{2,1,0:T(1,128)} %broadcast_in_dim.113), calls=%async_computation.22 | async-start | bytes 16384 | tf_op jit(solution)/shard_map/all_to_all | solution.py:27
  460.7 89.8 %collective-permute-start.9 = (f32[2,2,64,256]{3,2,1,0:T(8,128)}, f32[2,2,64,256]{3,2,1,0:T(8,128)S(1)}, u32[]{:S(2)}, u32[]{:S(2)}) collective-permute-start(f32[2,2,64,256]{3,2,1,0:T(8,128)} %get-tuple-element.35), channel_id=1, source_target_pairs={{16,0},{32,16},{48,32},{64,48},{80,64},{96,80},{112,96},{17,1},{33... | collective-permute-start | bytes 786440 | tf_op jit(solution)/shard_map/ppermute | solution.py:20
  469.3 11.4 %all-to-all-start.23 = ((f32[16,1,1024]{2,1,0:T(1,128)}), f32[16,1,1024]{2,1,0:T(1,128)S(1)}, u32[]{:S(2)}, u32[]{:S(2)}) async-start(f32[16,1,1024]{2,1,0:T(1,128)} %broadcast_in_dim.114), calls=%async_computation.23 | async-start | bytes 131072 | tf_op jit(solution)/shard_map/all_to_all | solution.py:27
  480.7 11.1 %all-to-all-start.24 = ((f32[16,8,128]{2,1,0:T(8,128)}), f32[16,8,128]{2,1,0:T(8,128)S(1)}, u32[]{:S(2)}, u32[]{:S(2)}) async-start(f32[16,8,128]{2,1,0:T(8,128)} %bitcast.145), calls=%async_computation.24 | async-start | bytes 131072 | tf_op jit(solution)/shard_map/all_to_all | solution.py:49
  494.4 10.8 %all-to-all-start.25 = ((f32[16,1,2]{2,1,0:T(1,128)}), f32[16,1,2]{2,1,0:T(1,128)S(1)}, u32[]{:S(2)}, u32[]{:S(2)}) async-start(f32[16,1,2]{2,1,0:T(1,128)} %broadcast_in_dim.115), calls=%async_computation.25 | async-start | bytes 16384 | tf_op jit(solution)/shard_map/all_to_all | solution.py:27
  499.2 51.4 %collective-permute-start.8 = (f32[2,2,64,256]{3,2,1,0:T(8,128)}, f32[2,2,64,256]{3,2,1,0:T(8,128)}, u32[]{:S(2)}, u32[]{:S(2)}) collective-permute-start(f32[2,2,64,256]{3,2,1,0:T(8,128)} %get-tuple-element.34), channel_id=1, source_target_pairs={{0,16},{16,32},{32,48},{48,64},{64,80},{80,96},{96,112},{1,17},{17... | collective-permute-start | bytes 786440 | tf_op jit(solution)/shard_map/ppermute | solution.py:17
  510.9 11.2 %all-to-all-start.26 = ((f32[16,1,1024]{2,1,0:T(1,128)}), f32[16,1,1024]{2,1,0:T(1,128)S(1)}, u32[]{:S(2)}, u32[]{:S(2)}) async-start(f32[16,1,1024]{2,1,0:T(1,128)} %broadcast_in_dim.216), calls=%async_computation.26 | async-start | bytes 131072 | tf_op jit(solution)/shard_map/all_to_all | solution.py:27
  522.1 11.1 %all-to-all-start.27 = ((f32[16,8,128]{2,1,0:T(8,128)}), f32[16,8,128]{2,1,0:T(8,128)S(1)}, u32[]{:S(2)}, u32[]{:S(2)}) async-start(f32[16,8,128]{2,1,0:T(8,128)} %bitcast.163), calls=%async_computation.27 | async-start | bytes 131072 | tf_op jit(solution)/shard_map/all_to_all | solution.py:49
  551.7 6.5 %collective-permute-start.11 = (f32[2,20,2,256]{3,2,1,0:T(2,128)S(1)}, f32[2,20,2,256]{3,2,1,0:T(2,128)S(1)}, u32[]{:S(2)}, u32[]{:S(2)}) collective-permute-start(f32[2,20,2,256]{3,2,1,0:T(2,128)S(1)} %get-tuple-element.31), channel_id=1, source_target_pairs={{1,0},{2,1},{3,2},{4,3},{5,4},{6,5},{7,6},{8,7},{9,8},{10,9},{11,1... | collective-permute-start | bytes 245768 | tf_op jit(solution)/shard_map/ppermute | solution.py:20
  555.7 8.4 %collective-permute-start.10 = (f32[2,20,2,256]{3,2,1,0:T(2,128)S(1)}, f32[2,20,2,256]{3,2,1,0:T(2,128)S(1)}, u32[]{:S(2)}, u32[]{:S(2)}) collective-permute-start(f32[2,20,2,256]{3,2,1,0:T(2,128)S(1)} %get-tuple-element.30), channel_id=1, source_target_pairs={{0,1},{1,2},{2,3},{3,4},{4,5},{5,6},{6,7},{7,8},{8,9},{9,10},{10,1... | collective-permute-start | bytes 245768 | tf_op jit(solution)/shard_map/ppermute | solution.py:17
  (45 other events, 442.1 us)
where the time goes:
time: 587 us; the launch traced here: 576 us
  starting transfers between devices  188 us (32%)
  waiting for transfers between devices  103 us (18%)
  blocking collectives  85.6 us (15%)
  other arithmetic  83.5 us (14%)
  local copies, waits for them, and re-layouts  69.9 us (12%)
  matrix products  25.7 us (4%)
  between operations  21.3 us (4%)
    all_to_all x13, starting transfers between devices, copy_for_each(): lax.all_to_all(jnp.broadcast_to(x[None], (length, *x.shape)), axis, 0, 0,...  65.3 us
    all_to_all x10, starting transfers between devices, summed_on_arrival(): blocks = lax.all_to_all(split_up(x, dim, length), axis, 0, 0, tiled=True)  50.7 us
    all_to_all x13, waiting for transfers between devices, copy_for_each(): lax.all_to_all(jnp.broadcast_to(x[None], (length, *x.shape)), axis, 0, 0,...  49.9 us
    all_gather x2, blocking collectives, body(): fracture_whole = lax.all_gather(fracture, 'frac', axis=0, tiled=True)  48.4 us
    psum x2, blocking collectives, body(): load = lax.psum(rows_part, 'mat')  26.5 us
    all_to_all x10, waiting for transfers between devices, summed_on_arrival(): blocks = lax.all_to_all(split_up(x, dim, length), axis, 0, 0, tiled=True)  24 us
    all_to_all x2, starting transfers between devices, body(): lax.all_to_all(flux_slots, ('mat', 'frac'), split_axis=0, concat_axis=0,...  16.9 us
    dot_general x8, matrix products, fracture_apply(): jnp.einsum('rtij,rtj->ri', tiles, blocks[tile_cols], precision=lax.Precis...  16.8 us
  transfers between devices with their start and end apart: 40, of which 25 were waited for; matrix products, arithmetic and copies ran while one was open for 26% of the time, Pallas kernels for 0%

commit v1 on v0

--- a/solution.py
+++ b/solution.py
@@ -7,6 +7,24 @@
 CG_ITERS = 3
 OUTER = 2
 relax_weight = 0.8
+
+
+def ring_gather(value, axis, dim):
+    ways, here, hop = (lax.axis_size(axis), lax.axis_index(axis), value.shape[dim])
+    dims = [n * ways if d == dim else n for d, n in enumerate(value.shape)]
+    full = lax.dynamic_update_slice_in_dim(
+        jnp.zeros(dims, value.dtype), value, here * hop, axis=dim
+    )
+    going_up = going_down = value
+    for far in range(1, ways // 2 + 1):
+        going_up = lax.ppermute(going_up, axis, [(d, (d + 1) % ways) for d in range(ways)])
+        full = lax.dynamic_update_slice_in_dim(full, going_up, (here - far) % ways * hop, axis=dim)
+        if 2 * far < ways:
+            going_down = lax.ppermute(going_down, axis, [(d, (d - 1) % ways) for d in range(ways)])
+            full = lax.dynamic_update_slice_in_dim(
+                full, going_down, (here + far) % ways * hop, axis=dim
+            )
+    return full
 
 
 def with_halo(block, sides, width):
@@ -184,7 +202,7 @@
             local_values, ("mat", "frac"), split_axis=0, concat_axis=0, tiled=True
         )
         trace = returned.reshape(-1)[place]
-        fracture_whole = lax.all_gather(fracture, "frac", axis=0, tiled=True)
+        fracture_whole = ring_gather(fracture, "frac", 0)
         flux = mortar_kappa * (trace - fracture_whole[mortar_frac])
         landed = jax.ops.segment_sum(flux, mortar_frac, num_segments=fracture_whole.shape[0])
         rows_part = summed_on_arrival(landed, "frac", 0)

time: 587 us -> 632 us (1.077)
  the two profiles are of different devices: /device:TPU:32 before, /device:TPU:24 now
where the time goes in v1:
time: 632 us; the launch traced here: 620 us
  starting transfers between devices  262 us (41%)
  waiting for transfers between devices  88.2 us (14%)
  other arithmetic  83.6 us (13%)
  local copies, waits for them, and re-layouts  80.3 us (13%)
  blocking collectives  58.7 us (9%)
  matrix products  24.9 us (4%)
  between operations  22.3 us (4%)
    all_to_all x11, starting transfers between devices, copy_for_each(): lax.all_to_all(jnp.broadcast_to(x[None], (length, *x.shape)), axis, 0, 0,...  66.1 us
    all_to_all x10, starting transfers between devices, summed_on_arrival(): blocks = lax.all_to_all(split_up(x, dim, length), axis, 0, 0, tiled=True)  61.7 us
    ppermute x16, starting transfers between devices, ring_gather(): lax.ppermute(going_up, axis, [(d, (d + 1) % ways) for d in range(ways)])  50.5 us
    all_to_all x11, waiting for transfers between devices, copy_for_each(): lax.all_to_all(jnp.broadcast_to(x[None], (length, *x.shape)), axis, 0, 0,...  33.8 us
    all_to_all x3, blocking collectives, copy_for_each(): lax.all_to_all(jnp.broadcast_to(x[None], (length, *x.shape)), axis, 0, 0,...  32.2 us
    psum x2, blocking collectives, body(): load = lax.psum(rows_part, 'mat')  26.5 us
    all_to_all x10, waiting for transfers between devices, summed_on_arrival(): blocks = lax.all_to_all(split_up(x, dim, length), axis, 0, 0, tiled=True)  22.5 us
    all_to_all x2, starting transfers between devices, body(): lax.all_to_all(local_values, ('mat', 'frac'), split_axis=0, concat_axis=0...  21.1 us
  transfers between devices with their start and end apart: 68, of which 29 were waited for; matrix products, arithmetic and copies ran while one was open for 27% of the time, Pallas kernels for 0%

profile of v1, /device:TPU:24, one launch (start us, length us, event | category | flops | bytes accessed | tf_op | source)
XLA Modules:
  0.0 619.9 jit_solution(16179446036425798801)
XLA Ops:
  7.8 10.3 %all-to-all-start = ((s32[128,1,8]{2,1,0:T(1,128)}), s32[128,1,8]{2,1,0:T(1,128)S(1)}, u32[]{:S(2)}, u32[]{:S(2)}) async-start(s32[128,1,8]{2,1,0:T(1,128)} %bitcast.4), calls=%async_computation | async-start | bytes 131072 | tf_op jit(solution)/shard_map/all_to_all | solution.py:158
  36.8 6.1 gather_fusion
  43.7 8.4 %all-to-all-start.1 = ((f32[128,1,8]{2,1,0:T(1,128)}), f32[128,1,8]{2,1,0:T(1,128)S(1)}, u32[]{:S(2)}, u32[]{:S(2)}) async-start(f32[128,1,8]{2,1,0:T(1,128)} %bitcast.6), calls=%async_computation.1 | async-start | bytes 131072 | tf_op jit(solution)/shard_map/all_to_all | solution.py:201
  57.8 4.1 collective-permute-start.8
  62.6 9.8 %all-to-all-start.5 = ((f32[16,1,1024]{2,1,0:T(1,128)}), f32[16,1,1024]{2,1,0:T(1,128)S(1)}, u32[]{:S(2)}, u32[]{:S(2)}) async-start(f32[16,1,1024]{2,1,0:T(1,128)} %broadcast_in_dim.103), calls=%async_computation.5 | async-start | bytes 131072 | tf_op jit(solution)/shard_map/all_to_all | solution.py:45
  78.3 4.1 collective-permute-start.12
  84.1 4.6 collective-permute-start.14
  101.3 10.3 %all-to-all-start.6 = ((f32[16,8,128]{2,1,0:T(8,128)}), f32[16,8,128]{2,1,0:T(8,128)S(1)}, u32[]{:S(2)}, u32[]{:S(2)}) async-start(f32[16,8,128]{2,1,0:T(8,128)} %bitcast.40), calls=%async_computation.6 | async-start | bytes 131072 | tf_op jit(solution)/shard_map/all_to_all | solution.py:67
  117.3 6.0 all-to-all-start.4
  129.0 12.4 %psum.14 = f32[1024]{0:T(1024)S(1)} all-reduce(f32[1024]{0:T(1024)S(1)} %reduce_sum.265), channel_id=1, replica_groups=mesh['mat'=8,'frac'=16] {'mat'}, use_global_device_ids=true, to_apply=%region_6.7 | all-reduce | flops 1024 | bytes 8192 | tf_op jit(solution)/shard_map/psum | solution.py:209
  142.1 5.4 all-to-all-start.7
  153.3 5.4 all-to-all-start.8
  166.4 10.7 %all_to_all.187 = f32[16,1,2]{2,1,0:T(1,128)S(1)} all-to-all(f32[16,1,2]{2,1,0:T(1,128)S(1)} %broadcast_in_dim.106), channel_id=1, replica_groups=mesh['mat'=8,'frac'=16] {'frac'}, dimensions={0} | all-to-all | bytes 256 | tf_op jit(solution)/shard_map/all_to_all | solution.py:45
  179.7 5.5 all-to-all-start.10
  191.0 5.4 all-to-all-start.11
  204.2 10.7 %all_to_all.188 = f32[16,1,2]{2,1,0:T(1,128)S(1)} all-to-all(f32[16,1,2]{2,1,0:T(1,128)S(1)} %broadcast_in_dim.108), channel_id=1, replica_groups=mesh['mat'=8,'frac'=16] {'frac'}, dimensions={0} | all-to-all | bytes 256 | tf_op jit(solution)/shard_map/all_to_all | solution.py:45
  221.0 5.4 all-to-all-start.13
  232.1 5.4 all-to-all-start.14
  245.9 5.3 all-to-all-start.15
  251.2 5.6 all-to-all-done.15
  266.8 6.5 %all-to-all-start.2 = ((f32[128,1,8]{2,1,0:T(1,128)}), f32[128,1,8]{2,1,0:T(1,128)S(1)}, u32[]{:S(2)}, u32[]{:S(2)}) async-start(f32[128,1,8]{2,1,0:T(1,128)} %bitcast.7), calls=%async_computation.2 | async-start | bytes 131072 | tf_op jit(solution)/shard_map/all_to_all | solution.py:217
  282.5 6.9 %scatter_custom_fusion.2 = f32[262144]{0:T(1024)} fusion(s32[1024]{0:T(1024)S(1)} %reshape.654, f32[1024]{0:T(1024)S(1)} %reshape.656, f32[]{:T(128)} %constant.163.clone.1), kind=kCustom, calls=%fused_computation.158 | custom fusion | flops 1024 | bytes 1048580 | tf_op jit(solution)/shard_map/scatter-add | solution.py:220
  300.2 4.1 collective-permute-start.29
  307.3 5.7 collective-permute-done.30
  320.1 6.0 collective-permute-start.17
  328.1 4.2 collective-permute-start.35
  333.7 6.0 all-to-all-start.18
  361.8 5.9 fusion.32
  368.9 4.6 fusion.66
  375.1 6.2 gather_fusion.3
  382.1 12.8 %all-to-all-start.3 = ((f32[128,1,8]{2,1,0:T(1,128)}), f32[128,1,8]{2,1,0:T(1,128)S(1)}, u32[]{:S(2)}, u32[]{:S(2)}) async-start(f32[128,1,8]{2,1,0:T(1,128)} %bitcast.25), calls=%async_computation.3 | async-start | bytes 131072 | tf_op jit(solution)/shard_map/all_to_all | solution.py:201
  407.6 7.7 %all-to-all-start.19 = ((f32[16,8,128]{2,1,0:T(8,128)}), f32[16,8,128]{2,1,0:T(8,128)S(1)}, u32[]{:S(2)}, u32[]{:S(2)}) async-start(f32[16,8,128]{2,1,0:T(8,128)} %bitcast.112), calls=%async_computation.19 | async-start | bytes 131072 | tf_op jit(solution)/shard_map/all_to_all | solution.py:67
  421.9 9.3 %all-to-all-start.16 = ((f32[128,1,8]{2,1,0:T(1,128)}), f32[128,1,8]{2,1,0:T(1,128)S(1)}, u32[]{:S(2)}, u32[]{:S(2)}) async-start(f32[128,1,8]{2,1,0:T(1,128)} %bitcast.96), calls=%async_computation.16 | async-start | bytes 131072 | tf_op jit(solution)/shard_map/all_to_all | solution.py:217
  439.5 5.4 all-to-all-start.17
  445.9 7.4 %scatter_custom_fusion.9 = f32[262144]{0:T(1024)} fusion(s32[1024]{0:T(1024)} %copy-done.44, f32[1024]{0:T(1024)S(1)} %reshape.712, f32[]{:T(128)} %constant.163.clone.1), kind=kCustom, calls=%fused_computation.156 | custom fusion | flops 1024 | bytes 1049088 | tf_op jit(solution)/shard_map/scatter-add | solution.py:220
  457.7 14.1 %psum.15 = f32[1024]{0:T(1024)S(1)} all-reduce(f32[1024]{0:T(1024)S(1)} %reduce_sum.279), channel_id=1, replica_groups=mesh['mat'=8,'frac'=16] {'mat'}, use_global_device_ids=true, to_apply=%region_28.29 | all-reduce | flops 1024 | bytes 8192 | tf_op jit(solution)/shard_map/psum | solution.py:209
  472.5 7.2 %all-to-all-start.20 = ((f32[16,1,1024]{2,1,0:T(1,128)}), f32[16,1,1024]{2,1,0:T(1,128)S(1)}, u32[]{:S(2)}, u32[]{:S(2)}) async-start(f32[16,1,1024]{2,1,0:T(1,128)} %broadcast_in_dim.112), calls=%async_computation.20 | async-start | bytes 131072 | tf_op jit(solution)/shard_map/all_to_all | solution.py:45
  485.5 5.4 all-to-all-start.21
  499.2 5.3 all-to-all-start.22
  505.9 4.3 all-to-all-done.22
  512.9 5.4 all-to-all-start.23
  524.0 5.4 all-to-all-start.24
  537.8 5.3 all-to-all-start.25
  544.4 4.3 all-to-all-done.25
  554.7 5.4 all-to-all-start.26
  565.8 5.4 all-to-all-start.27
  578.9 10.7 %all_to_all.189 = f32[16,1,2]{2,1,0:T(1,128)S(1)} all-to-all(f32[16,1,2]{2,1,0:T(1,128)S(1)} %broadcast_in_dim.217), channel_id=1, replica_groups=mesh['mat'=8,'frac'=16] {'frac'}, dimensions={0} | all-to-all | bytes 256 | tf_op jit(solution)/shard_map/all_to_all | solution.py:45
  602.1 5.7 collective-permute-done.41
  (436 shorter events, 274.2 us)
Async XLA Ops:
  0.6 28.8 %collective-permute-start = (f32[1024]{0:T(1024)}, f32[1024]{0:T(1024)S(1)}, u32[]{:S(2)}, u32[]{:S(2)}) collective-permute-start(f32[1024]{0:T(1024)} %param.25), channel_id=1, source_target_pairs={{0,1},{1,2},{2,3},{3,4},{4,5},{5,6},{6,7},{7,8},{8,9},{9,10},{10,1... | collective-permute-start | bytes 12296 | tf_op jit(solution)/shard_map/ppermute | solution.py:20
  2.3 28.9 %collective-permute-start.1 = (f32[1024]{0:T(1024)}, f32[1024]{0:T(1024)S(1)}, u32[]{:S(2)}, u32[]{:S(2)}) collective-permute-start(f32[1024]{0:T(1024)} %param.25), channel_id=1, source_target_pairs={{0,15},{1,0},{2,1},{3,2},{4,3},{5,4},{6,5},{7,6},{8,7},{9,8},{10,9... | collective-permute-start | bytes 12296 | tf_op jit(solution)/shard_map/ppermute | solution.py:23
  7.8 21.5 %all-to-all-start = ((s32[128,1,8]{2,1,0:T(1,128)}), s32[128,1,8]{2,1,0:T(1,128)S(1)}, u32[]{:S(2)}, u32[]{:S(2)}) async-start(s32[128,1,8]{2,1,0:T(1,128)} %bitcast.4), calls=%async_computation | async-start | bytes 131072 | tf_op jit(solution)/shard_map/all_to_all | solution.py:158
  20.6 325.0 %collective-permute-start.19 = (f32[5,2,64,256]{3,2,1,0:T(8,128)}, f32[5,2,64,256]{3,2,1,0:T(8,128)}, u32[]{:S(2)}, u32[]{:S(2)}) collective-permute-start(f32[5,2,64,256]{3,2,1,0:T(8,128)} %get-tuple-element.26), channel_id=1, source_target_pairs={{0,16},{16,32},{32,48},{48,64},{64,80},{80,96},{96,112},{1,17},{17... | collective-permute-start | bytes 1966088 | tf_op jit(solution)/shard_map/ppermute | solution.py:35
  31.2 20.8 %collective-permute-start.3 = (f32[1024]{0:T(1024)S(1)}, f32[1024]{0:T(1024)S(1)}, u32[]{:S(2)}, u32[]{:S(2)}) collective-permute-start(f32[1024]{0:T(1024)S(1)} %collective-permute-done.1), channel_id=1, source_target_pairs={{0,15},{1,0},{2,1},{3,2},{4,3},{5,4},{6,5},{7,6},{8,7},{9,8},{10,9... | collective-permute-start | bytes 12296 | tf_op jit(solution)/shard_map/ppermute | solution.py:23
  33.1 19.8 %collective-permute-start.4 = (f32[1024]{0:T(1024)S(1)}, f32[1024]{0:T(1024)S(1)}, u32[]{:S(2)}, u32[]{:S(2)}) collective-permute-start(f32[1024]{0:T(1024)S(1)} %collective-permute-done.2), channel_id=1, source_target_pairs={{0,1},{1,2},{2,3},{3,4},{4,5},{5,6},{6,7},{7,8},{8,9},{9,10},{10,1... | collective-permute-start | bytes 12296 | tf_op jit(solution)/shard_map/ppermute | solution.py:20
  43.7 18.3 %all-to-all-start.1 = ((f32[128,1,8]{2,1,0:T(1,128)}), f32[128,1,8]{2,1,0:T(1,128)S(1)}, u32[]{:S(2)}, u32[]{:S(2)}) async-start(f32[128,1,8]{2,1,0:T(1,128)} %bitcast.6), calls=%async_computation.1 | async-start | bytes 131072 | tf_op jit(solution)/shard_map/all_to_all | solution.py:201
  57.8 14.7 %collective-permute-start.7 = (f32[1024]{0:T(1024)S(1)}, f32[1024]{0:T(1024)S(1)}, u32[]{:S(2)}, u32[]{:S(2)}) collective-permute-start(f32[1024]{0:T(1024)S(1)} %collective-permute-done.5), channel_id=1, source_target_pairs={{0,15},{1,0},{2,1},{3,2},{4,3},{5,4},{6,5},{7,6},{8,7},{9,8},{10,9... | collective-permute-start | bytes 12296 | tf_op jit(solution)/shard_map/ppermute | solution.py:23
  57.8 15.7 %collective-permute-start.8 = (f32[1024]{0:T(1024)S(1)}, f32[1024]{0:T(1024)S(1)}, u32[]{:S(2)}, u32[]{:S(2)}) collective-permute-start(f32[1024]{0:T(1024)S(1)} %collective-permute-done.6), channel_id=1, source_target_pairs={{0,1},{1,2},{2,3},{3,4},{4,5},{5,6},{6,7},{7,8},{8,9},{9,10},{10,1... | collective-permute-start | bytes 12296 | tf_op jit(solution)/shard_map/ppermute | solution.py:20
  62.6 38.7 %all-to-all-start.5 = ((f32[16,1,1024]{2,1,0:T(1,128)}), f32[16,1,1024]{2,1,0:T(1,128)S(1)}, u32[]{:S(2)}, u32[]{:S(2)}) async-start(f32[16,1,1024]{2,1,0:T(1,128)} %broadcast_in_dim.103), calls=%async_computation.5 | async-start | bytes 131072 | tf_op jit(solution)/shard_map/all_to_all | solution.py:45
  84.1 13.5 %collective-permute-start.13 = (f32[1024]{0:T(1024)S(1)}, f32[1024]{0:T(1024)S(1)}, u32[]{:S(2)}, u32[]{:S(2)}) collective-permute-start(f32[1024]{0:T(1024)S(1)} %collective-permute-done.11), channel_id=1, source_target_pairs={{0,15},{1,0},{2,1},{3,2},{4,3},{5,4},{6,5},{7,6},{8,7},{9,8},{10,9... | collective-permute-start | bytes 12296 | tf_op jit(solution)/shard_map/ppermute | solution.py:23
  84.1 13.8 %collective-permute-start.14 = (f32[1024]{0:T(1024)S(1)}, f32[1024]{0:T(1024)S(1)}, u32[]{:S(2)}, u32[]{:S(2)}) collective-permute-start(f32[1024]{0:T(1024)S(1)} %collective-permute-done.12), channel_id=1, source_target_pairs={{0,1},{1,2},{2,3},{3,4},{4,5},{5,6},{6,7},{7,8},{8,9},{9,10},{10,1... | collective-permute-start | bytes 12296 | tf_op jit(solution)/shard_map/ppermute | solution.py:20
  101.3 16.0 %all-to-all-start.6 = ((f32[16,8,128]{2,1,0:T(8,128)}), f32[16,8,128]{2,1,0:T(8,128)S(1)}, u32[]{:S(2)}, u32[]{:S(2)}) async-start(f32[16,8,128]{2,1,0:T(8,128)} %bitcast.40), calls=%async_computation.6 | async-start | bytes 131072 | tf_op jit(solution)/shard_map/all_to_all | solution.py:67
  117.3 11.7 %all-to-all-start.4 = ((f32[16,1,1024]{2,1,0:T(1,128)}), f32[16,1,1024]{2,1,0:T(1,128)S(1)}, u32[]{:S(2)}, u32[]{:S(2)}) async-start(f32[16,1,1024]{2,1,0:T(1,128)} %bitcast.26), calls=%async_computation.4 | async-start | bytes 131072 | tf_op jit(solution)/shard_map/all_to_all | solution.py:67
  142.1 11.1 %all-to-all-start.7 = ((f32[16,1,1024]{2,1,0:T(1,128)}), f32[16,1,1024]{2,1,0:T(1,128)S(1)}, u32[]{:S(2)}, u32[]{:S(2)}) async-start(f32[16,1,1024]{2,1,0:T(1,128)} %broadcast_in_dim.105), calls=%async_computation.7 | async-start | bytes 131072 | tf_op jit(solution)/shard_map/all_to_all | solution.py:45
  153.3 11.1 %all-to-all-start.8 = ((f32[16,8,128]{2,1,0:T(8,128)}), f32[16,8,128]{2,1,0:T(8,128)S(1)}, u32[]{:S(2)}, u32[]{:S(2)}) async-start(f32[16,8,128]{2,1,0:T(8,128)} %bitcast.55), calls=%async_computation.8 | async-start | bytes 131072 | tf_op jit(solution)/shard_map/all_to_all | solution.py:67
  179.7 11.3 %all-to-all-start.10 = ((f32[16,1,1024]{2,1,0:T(1,128)}), f32[16,1,1024]{2,1,0:T(1,128)S(1)}, u32[]{:S(2)}, u32[]{:S(2)}) async-start(f32[16,1,1024]{2,1,0:T(1,128)} %broadcast_in_dim.107), calls=%async_computation.10 | async-start | bytes 131072 | tf_op jit(solution)/shard_map/all_to_all | solution.py:45
  191.0 11.1 %all-to-all-start.11 = ((f32[16,8,128]{2,1,0:T(8,128)}), f32[16,8,128]{2,1,0:T(8,128)S(1)}, u32[]{:S(2)}, u32[]{:S(2)}) async-start(f32[16,8,128]{2,1,0:T(8,128)} %bitcast.73), calls=%async_computation.11 | async-start | bytes 131072 | tf_op jit(solution)/shard_map/all_to_all | solution.py:67
  221.0 11.1 %all-to-all-start.13 = ((f32[16,1,1024]{2,1,0:T(1,128)}), f32[16,1,1024]{2,1,0:T(1,128)S(1)}, u32[]{:S(2)}, u32[]{:S(2)}) async-start(f32[16,1,1024]{2,1,0:T(1,128)} %broadcast_in_dim.109), calls=%async_computation.13 | async-start | bytes 131072 | tf_op jit(solution)/shard_map/all_to_all | solution.py:45
  232.1 11.1 %all-to-all-start.14 = ((f32[16,8,128]{2,1,0:T(8,128)}), f32[16,8,128]{2,1,0:T(8,128)S(1)}, u32[]{:S(2)}, u32[]{:S(2)}) async-start(f32[16,8,128]{2,1,0:T(8,128)} %bitcast.91), calls=%async_computation.14 | async-start | bytes 131072 | tf_op jit(solution)/shard_map/all_to_all | solution.py:67
  245.9 10.9 %all-to-all-start.15 = ((f32[16,1,2]{2,1,0:T(1,128)}), f32[16,1,2]{2,1,0:T(1,128)S(1)}, u32[]{:S(2)}, u32[]{:S(2)}) async-start(f32[16,1,2]{2,1,0:T(1,128)} %broadcast_in_dim.110), calls=%async_computation.15 | async-start | bytes 16384 | tf_op jit(solution)/shard_map/all_to_all | solution.py:45
  261.5 12.7 %collective-permute-start.23 = (f32[1024]{0:T(1024)S(1)}, f32[1024]{0:T(1024)S(1)}, u32[]{:S(2)}, u32[]{:S(2)}) collective-permute-start(f32[1024]{0:T(1024)S(1)} %get-tuple-element.17), channel_id=1, source_target_pairs={{0,1},{1,2},{2,3},{3,4},{4,5},{5,6},{6,7},{7,8},{8,9},{9,10},{10,1... | collective-permute-start | bytes 12296 | tf_op jit(solution)/shard_map/ppermute | solution.py:20
  266.8 14.7 %all-to-all-start.2 = ((f32[128,1,8]{2,1,0:T(1,128)}), f32[128,1,8]{2,1,0:T(1,128)S(1)}, u32[]{:S(2)}, u32[]{:S(2)}) async-start(f32[128,1,8]{2,1,0:T(1,128)} %bitcast.7), calls=%async_computation.2 | async-start | bytes 131072 | tf_op jit(solution)/shard_map/all_to_all | solution.py:217
  273.3 18.7 %collective-permute-start.24 = (f32[1024]{0:T(1024)S(1)}, f32[1024]{0:T(1024)S(1)}, u32[]{:S(2)}, u32[]{:S(2)}) collective-permute-start(f32[1024]{0:T(1024)S(1)} %get-tuple-element.17), channel_id=1, source_target_pairs={{0,15},{1,0},{2,1},{3,2},{4,3},{5,4},{6,5},{7,6},{8,7},{9,8},{10,9... | collective-permute-start | bytes 12296 | tf_op jit(solution)/shard_map/ppermute | solution.py:23
  274.2 18.5 %collective-permute-start.25 = (f32[1024]{0:T(1024)S(1)}, f32[1024]{0:T(1024)S(1)}, u32[]{:S(2)}, u32[]{:S(2)}) collective-permute-start(f32[1024]{0:T(1024)S(1)} %collective-permute-done.23), channel_id=1, source_target_pairs={{0,1},{1,2},{2,3},{3,4},{4,5},{5,6},{6,7},{7,8},{8,9},{9,10},{10,1... | collective-permute-start | bytes 12296 | tf_op jit(solution)/shard_map/ppermute | solution.py:20
  297.4 16.2 %collective-permute-start.15 = (f32[2,2,64,256]{3,2,1,0:T(8,128)S(1)}, f32[2,2,64,256]{3,2,1,0:T(8,128)S(1)}, u32[]{:S(2)}, u32[]{:S(2)}) collective-permute-start(f32[2,2,64,256]{3,2,1,0:T(8,128)S(1)} %get-tuple-element.38), channel_id=1, source_target_pairs={{0,16},{16,32},{32,48},{48,64},{64,80},{80,96},{96,112},{1,17},{17... | collective-permute-start | bytes 786440 | tf_op jit(solution)/shard_map/ppermute | solution.py:35
  298.7 20.6 %collective-permute-start.16 = (f32[2,2,64,256]{3,2,1,0:T(8,128)S(1)}, f32[2,2,64,256]{3,2,1,0:T(8,128)S(1)}, u32[]{:S(2)}, u32[]{:S(2)}) collective-permute-start(f32[2,2,64,256]{3,2,1,0:T(8,128)S(1)} %get-tuple-element.39), channel_id=1, source_target_pairs={{16,0},{32,16},{48,32},{64,48},{80,64},{96,80},{112,96},{17,1},{33... | collective-permute-start | bytes 786440 | tf_op jit(solution)/shard_map/ppermute | solution.py:38
  305.8 39.8 %collective-permute-start.20 = (f32[5,2,64,256]{3,2,1,0:T(8,128)}, f32[5,2,64,256]{3,2,1,0:T(8,128)}, u32[]{:S(2)}, u32[]{:S(2)}) collective-permute-start(f32[5,2,64,256]{3,2,1,0:T(8,128)} %get-tuple-element.27), channel_id=1, source_target_pairs={{16,0},{32,16},{48,32},{64,48},{80,64},{96,80},{112,96},{17,1},{33... | collective-permute-start | bytes 1966088 | tf_op jit(solution)/shard_map/ppermute | solution.py:38
  320.1 20.6 %collective-permute-start.17 = (f32[2,20,2,256]{3,2,1,0:T(2,128)}, f32[2,20,2,256]{3,2,1,0:T(2,128)}, u32[]{:S(2)}, u32[]{:S(2)}) collective-permute-start(f32[2,20,2,256]{3,2,1,0:T(2,128)} %get-tuple-element.34), channel_id=1, source_target_pairs={{0,1},{1,2},{2,3},{3,4},{4,5},{5,6},{6,7},{7,8},{8,9},{9,10},{10,1... | collective-permute-start | bytes 245768 | tf_op jit(solution)/shard_map/ppermute | solution.py:35
  326.2 17.8 %collective-permute-start.18 = (f32[2,20,2,256]{3,2,1,0:T(2,128)}, f32[2,20,2,256]{3,2,1,0:T(2,128)}, u32[]{:S(2)}, u32[]{:S(2)}) collective-permute-start(f32[2,20,2,256]{3,2,1,0:T(2,128)} %get-tuple-element.35), channel_id=1, source_target_pairs={{1,0},{2,1},{3,2},{4,3},{5,4},{6,5},{7,6},{8,7},{9,8},{10,9},{11,1... | collective-permute-start | bytes 245768 | tf_op jit(solution)/shard_map/ppermute | solution.py:38
  328.1 11.6 %collective-permute-start.35 = (f32[1024]{0:T(1024)}, f32[1024]{0:T(1024)}, u32[]{:S(2)}, u32[]{:S(2)}) collective-permute-start(f32[1024]{0:T(1024)} %collective-permute-done.33), channel_id=1, source_target_pairs={{0,1},{1,2},{2,3},{3,4},{4,5},{5,6},{6,7},{7,8},{8,9},{9,10},{10,1... | collective-permute-start | bytes 12296 | tf_op jit(solution)/shard_map/ppermute | solution.py:20
  333.7 48.4 %all-to-all-start.18 = ((f32[16,1,1024]{2,1,0:T(1,128)}), f32[16,1,1024]{2,1,0:T(1,128)S(1)}, u32[]{:S(2)}, u32[]{:S(2)}) async-start(f32[16,1,1024]{2,1,0:T(1,128)} %broadcast_in_dim.111), calls=%async_computation.18 | async-start | bytes 131072 | tf_op jit(solution)/shard_map/all_to_all | solution.py:45
  339.8 62.4 %collective-permute-start.36 = (f32[1024]{0:T(1024)}, f32[1024]{0:T(1024)}, u32[]{:S(2)}, u32[]{:S(2)}) collective-permute-start(f32[1024]{0:T(1024)} %copy-done.65), channel_id=1, source_target_pairs={{0,15},{1,0},{2,1},{3,2},{4,3},{5,4},{6,5},{7,6},{8,7},{9,8},{10,9... | collective-permute-start | bytes 12296 | tf_op jit(solution)/shard_map/ppermute | solution.py:23
  340.7 62.3 %collective-permute-start.37 = (f32[1024]{0:T(1024)}, f32[1024]{0:T(1024)}, u32[]{:S(2)}, u32[]{:S(2)}) collective-permute-start(f32[1024]{0:T(1024)} %collective-permute-done.35), channel_id=1, source_target_pairs={{0,1},{1,2},{2,3},{3,4},{4,5},{5,6},{6,7},{7,8},{8,9},{9,10},{10,1... | collective-permute-start | bytes 12296 | tf_op jit(solution)/shard_map/ppermute | solution.py:20
  382.1 25.5 %all-to-all-start.3 = ((f32[128,1,8]{2,1,0:T(1,128)}), f32[128,1,8]{2,1,0:T(1,128)S(1)}, u32[]{:S(2)}, u32[]{:S(2)}) async-start(f32[128,1,8]{2,1,0:T(1,128)} %bitcast.25), calls=%async_computation.3 | async-start | bytes 131072 | tf_op jit(solution)/shard_map/all_to_all | solution.py:201
  407.6 14.3 %all-to-all-start.19 = ((f32[16,8,128]{2,1,0:T(8,128)}), f32[16,8,128]{2,1,0:T(8,128)S(1)}, u32[]{:S(2)}, u32[]{:S(2)}) async-start(f32[16,8,128]{2,1,0:T(8,128)} %bitcast.112), calls=%async_computation.19 | async-start | bytes 131072 | tf_op jit(solution)/shard_map/all_to_all | solution.py:67
  421.9 17.6 %all-to-all-start.16 = ((f32[128,1,8]{2,1,0:T(1,128)}), f32[128,1,8]{2,1,0:T(1,128)S(1)}, u32[]{:S(2)}, u32[]{:S(2)}) async-start(f32[128,1,8]{2,1,0:T(1,128)} %bitcast.96), calls=%async_computation.16 | async-start | bytes 131072 | tf_op jit(solution)/shard_map/all_to_all | solution.py:217
  439.5 18.2 %all-to-all-start.17 = ((f32[16,1,1024]{2,1,0:T(1,128)}), f32[16,1,1024]{2,1,0:T(1,128)S(1)}, u32[]{:S(2)}, u32[]{:S(2)}) async-start(f32[16,1,1024]{2,1,0:T(1,128)} %bitcast.99), calls=%async_computation.17 | async-start | bytes 131072 | tf_op jit(solution)/shard_map/all_to_all | solution.py:67
  472.5 12.9 %all-to-all-start.20 = ((f32[16,1,1024]{2,1,0:T(1,128)}), f32[16,1,1024]{2,1,0:T(1,128)S(1)}, u32[]{:S(2)}, u32[]{:S(2)}) async-start(f32[16,1,1024]{2,1,0:T(1,128)} %broadcast_in_dim.112), calls=%async_computation.20 | async-start | bytes 131072 | tf_op jit(solution)/shard_map/all_to_all | solution.py:45
  485.5 11.1 %all-to-all-start.21 = ((f32[16,8,128]{2,1,0:T(8,128)}), f32[16,8,128]{2,1,0:T(8,128)S(1)}, u32[]{:S(2)}, u32[]{:S(2)}) async-start(f32[16,8,128]{2,1,0:T(8,128)} %bitcast.127), calls=%async_computation.21 | async-start | bytes 131072 | tf_op jit(solution)/shard_map/all_to_all | solution.py:67
  499.2 10.9 %all-to-all-start.22 = ((f32[16,1,2]{2,1,0:T(1,128)}), f32[16,1,2]{2,1,0:T(1,128)S(1)}, u32[]{:S(2)}, u32[]{:S(2)}) async-start(f32[16,1,2]{2,1,0:T(1,128)} %broadcast_in_dim.113), calls=%async_computation.22 | async-start | bytes 16384 | tf_op jit(solution)/shard_map/all_to_all | solution.py:45
  504.6 89.6 %collective-permute-start.38 = (f32[2,2,64,256]{3,2,1,0:T(8,128)}, f32[2,2,64,256]{3,2,1,0:T(8,128)S(1)}, u32[]{:S(2)}, u32[]{:S(2)}) collective-permute-start(f32[2,2,64,256]{3,2,1,0:T(8,128)} %get-tuple-element.36), channel_id=1, source_target_pairs={{0,16},{16,32},{32,48},{48,64},{64,80},{80,96},{96,112},{1,17},{17... | collective-permute-start | bytes 786440 | tf_op jit(solution)/shard_map/ppermute | solution.py:35
  512.9 11.1 %all-to-all-start.23 = ((f32[16,1,1024]{2,1,0:T(1,128)}), f32[16,1,1024]{2,1,0:T(1,128)S(1)}, u32[]{:S(2)}, u32[]{:S(2)}) async-start(f32[16,1,1024]{2,1,0:T(1,128)} %broadcast_in_dim.114), calls=%async_computation.23 | async-start | bytes 131072 | tf_op jit(solution)/shard_map/all_to_all | solution.py:45
  524.0 11.1 %all-to-all-start.24 = ((f32[16,8,128]{2,1,0:T(8,128)}), f32[16,8,128]{2,1,0:T(8,128)S(1)}, u32[]{:S(2)}, u32[]{:S(2)}) async-start(f32[16,8,128]{2,1,0:T(8,128)} %bitcast.145), calls=%async_computation.24 | async-start | bytes 131072 | tf_op jit(solution)/shard_map/all_to_all | solution.py:67
  537.8 10.9 %all-to-all-start.25 = ((f32[16,1,2]{2,1,0:T(1,128)}), f32[16,1,2]{2,1,0:T(1,128)S(1)}, u32[]{:S(2)}, u32[]{:S(2)}) async-start(f32[16,1,2]{2,1,0:T(1,128)} %broadcast_in_dim.115), calls=%async_computation.25 | async-start | bytes 16384 | tf_op jit(solution)/shard_map/all_to_all | solution.py:45
  543.1 51.0 %collective-permute-start.39 = (f32[2,2,64,256]{3,2,1,0:T(8,128)}, f32[2,2,64,256]{3,2,1,0:T(8,128)}, u32[]{:S(2)}, u32[]{:S(2)}) collective-permute-start(f32[2,2,64,256]{3,2,1,0:T(8,128)} %get-tuple-element.37), channel_id=1, source_target_pairs={{16,0},{32,16},{48,32},{64,48},{80,64},{96,80},{112,96},{17,1},{33... | collective-permute-start | bytes 786440 | tf_op jit(solution)/shard_map/ppermute | solution.py:38
  554.7 11.1 %all-to-all-start.26 = ((f32[16,1,1024]{2,1,0:T(1,128)}), f32[16,1,1024]{2,1,0:T(1,128)S(1)}, u32[]{:S(2)}, u32[]{:S(2)}) async-start(f32[16,1,1024]{2,1,0:T(1,128)} %broadcast_in_dim.216), calls=%async_computation.26 | async-start | bytes 131072 | tf_op jit(solution)/shard_map/all_to_all | solution.py:45
  565.8 11.1 %all-to-all-start.27 = ((f32[16,8,128]{2,1,0:T(8,128)}), f32[16,8,128]{2,1,0:T(8,128)S(1)}, u32[]{:S(2)}, u32[]{:S(2)}) async-start(f32[16,8,128]{2,1,0:T(8,128)} %bitcast.163), calls=%async_computation.27 | async-start | bytes 131072 | tf_op jit(solution)/shard_map/all_to_all | solution.py:67
  (92 other events, 1756.1 us)
